TPU v7x, 32 devices: a whole 2x2x4 slice. The times are simulated.
32 devices in a mesh: grp: 2 (over y), seq: 4 (over x, core), lab: 4 (over z).
Axes of the slice: x: 2, y: 2, z: 4, core: 2. Of those that a mesh axis runs over, the one named last changes fastest.
Arguments:
- hidden: bfloat16 [6144, 4096], P(('grp', 'seq'), 'lab'), parts along dimension 0, may hold values from -6 to 6
- proj_weight: bfloat16 [4096, 256], P('lab'), may hold values from -0.09375 to 0.09375
- queries: bfloat16 [9216, 256], P('lab'), may hold values from -0.25 to 0.25
- code_weight: bfloat16 [9216, 256], P('lab'), may hold values from -4 to 4
- code_bias: float32 [9216], P('lab'), may hold values from -0.5 to 0.5
- labels: int32 [4, 9216], P('grp', 'lab'), parts along dimension 0, may hold values 0 or 1
- code_counts: int32 [8, 9216], P(('grp', 'seq'), 'lab'), parts along dimension 0, may hold values from 0 to 119, as said below
Outputs:
- note_loss: float32 [4], P('grp'), parts along dimension 0
- grad_hidden: bfloat16 [6144, 4096], P(('grp', 'seq'), 'lab'), parts along dimension 0
- grad_proj: bfloat16 [8192, 256], P(('grp', 'lab', 'seq')), parts along dimension 0
- grad_queries: bfloat16 [18432, 256], P(('grp', 'lab', 'seq')), parts along dimension 0
- grad_code_weight: bfloat16 [18432, 256], P(('grp', 'lab', 'seq')), parts along dimension 0
- grad_bias: float32 [18432], P(('grp', 'lab')), parts along dimension 0
There are 2 independent parts, one for each index of `grp`. A program takes and returns all parts, laid end to end along the dimension named above; an argument that names none is the same for every part. Nothing has to cross between parts.
Inputs may be any that keep to these rules, and one draw needn't show every extreme that they name: `code_counts`: entry (i, c) counts the occurrences of code c in the part of the training corpus read by loader i.
All inputs are finite; a program needn't handle non-finite values. No bound on the sum of `labels` on one device may be relied on, other than what follows from the above.
Results may differ from a plain program's by a relative error of at most 0.025.
Values may be sent and summed in bfloat16 or wider, within the bound.
A program may use at most 64 MiB of HBM per device.

v0:
```python
import math
import jax
import jax.numpy as jnp
from jax import lax
from jax.sharding import PartitionSpec as P

balance_beta = 0.9999


def focal_loss(logit, target):
    prob = jax.nn.sigmoid(logit)
    return -(
        target * (1.0 - prob) * (1.0 - prob) * jax.nn.log_sigmoid(logit)
        + (1.0 - target) * prob * prob * jax.nn.log_sigmoid(-logit)
    )


def rounded(value):
    return lax.optimization_barrier(value.astype(jnp.bfloat16)).astype(jnp.float32)


def per_device(hidden, proj_weight, queries, code_weight, code_bias, labels, code_counts):
    lab_count = lax.axis_size("lab")
    seq_count = lax.axis_size("seq")
    note_count = labels.shape[0]
    all_codes = queries.shape[0] * lab_count
    pre_part = lax.psum_scatter(
        jnp.dot(hidden, proj_weight, preferred_element_type=jnp.float32).astype(jnp.bfloat16),
        "lab",
        scatter_dimension=0,
        tiled=True,
    ).astype(jnp.float32)
    latent_share = jnp.tanh(pre_part).astype(jnp.bfloat16)
    latent = lax.all_gather(latent_share, "lab", axis=0, tiled=True)
    scores = jnp.einsum("te,ce->tc", latent, queries, preferred_element_type=jnp.float32)
    values = jnp.einsum("te,ce->tc", latent, code_weight, preferred_element_type=jnp.float32)
    weights = jnp.exp(scores)
    note_here = lax.axis_index("seq") * note_count // seq_count
    note_pick = (jnp.arange(note_count, dtype=jnp.int32) == note_here).astype(jnp.float32)[:, None]
    den_local = jnp.sum(weights, 0)[None, :]
    num_local = jnp.sum(weights * values, 0)[None, :]
    counts_local = jnp.sum(code_counts.astype(jnp.float32), 0)
    denominator, numerator, counted = (
        lax.psum((note_pick * den_local).astype(jnp.bfloat16), "seq").astype(jnp.float32),
        lax.psum((note_pick * num_local).astype(jnp.bfloat16), "seq").astype(jnp.float32),
        lax.psum(counts_local.astype(jnp.bfloat16), "seq").astype(jnp.float32),
    )
    mean_value = numerator / denominator
    logits = mean_value + code_bias[None, :]
    occurrences = 1.0 + counted
    class_weight = (1.0 - balance_beta) / -jnp.expm1(occurrences * math.log(balance_beta))
    targets = labels.astype(jnp.float32)
    focal_value, pullback = jax.vjp(lambda point: focal_loss(point, targets), logits)
    focal_grad = pullback(jnp.ones_like(logits))[0]
    weight_total, weighted_loss = lax.psum(
        (jnp.sum(class_weight), jnp.sum(focal_value * class_weight[None, :], 1)), "lab"
    )
    factor = all_codes / weight_total
    note_loss = factor * weighted_loss
    logit_grad = factor * class_weight[None, :] * focal_grad
    grad_bias = jnp.sum(logit_grad, 0)
    grad_here = jnp.sum(note_pick * logit_grad, 0)[None, :]
    den_here = jnp.sum(note_pick * denominator, 0)[None, :]
    mean_here = jnp.sum(note_pick * mean_value, 0)[None, :]
    value_part = weights / den_here * grad_here
    score_part = value_part * (values - mean_here)
    value_grad = value_part.astype(jnp.bfloat16)
    score_grad = score_part.astype(jnp.bfloat16)
    first = jnp.dot(score_grad, queries, preferred_element_type=jnp.float32)
    grad_share = lax.psum_scatter(
        (first + jnp.dot(value_grad, code_weight, preferred_element_type=jnp.float32)).astype(
            jnp.bfloat16
        ),
        "lab",
        scatter_dimension=0,
        tiled=True,
    ).astype(jnp.float32)
    share_wide = latent_share.astype(jnp.float32)
    pre_share_grad = (grad_share * (1.0 - share_wide * share_wide)).astype(jnp.bfloat16)
    pre_grad = lax.all_gather(pre_share_grad, "lab", axis=0, tiled=True)
    grad_hidden = jnp.einsum(
        "te,de->td", pre_grad, proj_weight, preferred_element_type=jnp.float32
    ).astype(jnp.bfloat16)
    proj_part = jnp.einsum("td,te->de", hidden, pre_grad, preferred_element_type=jnp.float32)
    query_part = jnp.einsum("tc,te->ce", score_grad, latent, preferred_element_type=jnp.float32)
    weight_part = jnp.einsum("tc,te->ce", value_grad, latent, preferred_element_type=jnp.float32)
    query_sum, weight_sum, proj_sum = (
        lax.psum_scatter(
            rounded(query_part).astype(jnp.bfloat16), "seq", scatter_dimension=0, tiled=True
        ).astype(jnp.float32),
        lax.psum_scatter(
            rounded(weight_part).astype(jnp.bfloat16), "seq", scatter_dimension=0, tiled=True
        ).astype(jnp.float32),
        lax.psum_scatter(
            rounded(proj_part).astype(jnp.bfloat16), "seq", scatter_dimension=0, tiled=True
        ).astype(jnp.float32),
    )
    return (
        note_loss,
        grad_hidden,
        proj_sum.astype(jnp.bfloat16),
        query_sum.astype(jnp.bfloat16),
        weight_sum.astype(jnp.bfloat16),
        grad_bias,
    )


def solution(mesh):
    placed = (
        P(("grp", "seq"), "lab"),
        P("lab", None),
        P("lab", None),
        P("lab", None),
        P("lab"),
        P("grp", "lab"),
        P(("grp", "seq"), "lab"),
    )
    return jax.shard_map(
        per_device,
        mesh=mesh,
        in_specs=placed,
        out_specs=(
            P("grp"),
            P(("grp", "seq"), "lab"),
            P(("grp", "lab", "seq"), None),
            P(("grp", "lab", "seq"), None),
            P(("grp", "lab", "seq"), None),
            P(("grp", "lab")),
        ),
        check_vma=False,
    )
```

profile of v0, /device:TPU:0, one launch (start us, length us, event | category | flops | bytes accessed | tf_op | source)
XLA Modules:
  0.0 211.3 jit_solution(14797629354521924660)
XLA Ops:
  7.2 1.4 copy-done
  8.6 2.4 %convolution_convert_fusion.4 = bf16[768,256]{1,0:T(8,128)(2,1)} fusion(bf16[768,1024]{1,0:T(8,128)(2,1)S(1)} %copy-done, bf16[1024,256]{1,0:T(8,128)(2,1)} %param.9), kind=kOutput, calls=%fused_computation.11 | convolution fusion | flops 402849792 | bytes 2490368 | tf_op jit(solution)/shard_map/dot_general | solution.py:28
  11.0 0.7 convert_reduce_fusion
  11.8 22.6 %reduce-scatter.6.cloned.1.call-done = bf16[192,256]{1,0:T(8,128)(2,1)} async-done(((bf16[768,256]{1,0:T(8,128)(2,1)}), bf16[192,256]{1,0:T(8,128)(2,1)}) %reduce-scatter.6.cloned.1.call-update) | async-done | bytes 98320 | tf_op jit(solution)/shard_map/reduce_scatter | solution.py:27
  34.4 0.9 tanh_convert_fusion
  35.3 14.8 %all_gather.6 = bf16[768,256]{1,0:T(8,128)(2,1)S(1)} all-gather(bf16[192,256]{1,0:T(8,128)(2,1)S(1)} %tanh_convert_fusion), channel_id=1, replica_groups=mesh['grp'=2,'seq'=4,'lab'=4] {'lab'}, dimensions={0}, use_global_device_ids=true | all-gather | bytes 491520 | tf_op jit(solution)/shard_map/all_gather | solution.py:34
  50.2 2.5 %fusion.17 = f32[768,2304]{1,0:T(8,128)S(1)} fusion(bf16[768,256]{1,0:T(8,128)(2,1)S(1)} %all_gather.6, bf16[2304,256]{1,0:T(8,128)(2,1)} %param.10), kind=kOutput, calls=%fused_computation.52 | convolution fusion | flops 905969664 | bytes 8650752 | tf_op jit(solution)/shard_map/te,ce->tc/dot_general | solution.py:35
  52.7 4.8 %multiply_reduce_fusion = (f32[2304]{0:T(1024)S(1)}, f32[2304]{0:T(1024)S(1)}, f32[768,2304]{1,0:T(8,128)}) fusion(f32[768,2304]{1,0:T(8,128)S(1)} %fusion.17, bf16[768,256]{1,0:T(8,128)(2,1)S(1)} %all_gather.6, bf16[2304,256]{1,0:T(8,128)(2,1)S(1)} %copy-done.4), kind=kOutput, calls=%fused_computation.2 | convolution fusion | flops 911273472 | bytes 15747072 | tf_op jit(solution)/shard_map/te,ce->tc/dot_general | solution.py:36
  57.5 0.2 copy-done.1
  57.6 0.1 multiply_convert_fusion.3
  57.7 10.3 %all-reduce = (bf16[2304]{0:T(1024)(128)(2,1)S(1)}, bf16[2,2304]{1,0:T(2,128)(2,1)S(1)}, bf16[2,2304]{1,0:T(2,128)(2,1)S(1)}) all-reduce(bf16[2304]{0:T(1024)(128)(2,1)S(1)} %convert_reduce_fusion, bf16[2,2304]{1,0:T(2,128)(2,1)S(1)} %get-tuple-element.39, ...), channel_id=1, replica_groups=mesh['grp'=2,'seq'=4,'lab'=4] {'seq'}, use_global_device_ids=true, to_apply=%region_0.0 | all-reduce | flops 11520 | bytes 46080 | tf_op jit(solution)/shard_map/psum | solution.py:46
  68.0 0.6 negate_divide_fusion
  68.6 9.0 %psum.36 = f32[]{:T(128)} all-reduce(f32[]{:T(128)} %get-tuple-element.37), channel_id=1, replica_groups=mesh['grp'=2,'seq'=4,'lab'=4] {'lab'}, use_global_device_ids=true, to_apply=%region_2.3 | all-reduce | flops 1 | bytes 8 | tf_op jit(solution)/shard_map/psum | solution.py:55
  78.3 0.2 fusion.14
  78.5 0.8 fusion.16
  79.4 6.0 %fusion = (bf16[768,2304]{1,0:T(8,128)(2,1)S(1)}, bf16[768,2304]{1,0:T(8,128)(2,1)S(1)}) fusion(f32[2304]{0:T(1024)S(1)} %get-tuple-element.23, f32[2304]{0:T(1024)S(1)} %get-tuple-element.26, f32[768,2304]{1,0:T(8,128)} %copy-done.1, f32[768,2304]{1,0:T(8,128)} %get-tuple-element.40, f32[2304]{0:T(1024)S(1)} %get-tuple-element.28), kind=kLoop, calls=%fused_computation.6 | loop fusion | flops 10616832 | bytes 21261312 | tf_op jit(solution)/shard_map/convert_element_type | solution.py:67
  85.4 1.8 copy-done.3
  87.2 1.1 fusion.18
  88.3 1.8 fusion.1
  90.2 20.2 %reduce-scatter.8.cloned.1.call-done = bf16[192,256]{1,0:T(8,128)(2,1)} async-done(((bf16[768,256]{1,0:T(8,128)(2,1)}), bf16[192,256]{1,0:T(8,128)(2,1)}) %reduce-scatter.8.cloned.1.call-update) | async-done | bytes 98320 | tf_op jit(solution)/shard_map/reduce_scatter | solution.py:70
  110.4 0.9 multiply_convert_fusion.1
  111.3 14.8 %all_gather.7 = bf16[768,256]{1,0:T(8,128)(2,1)S(1)} all-gather(bf16[192,256]{1,0:T(8,128)(2,1)S(1)} %multiply_convert_fusion.1), channel_id=1, replica_groups=mesh['grp'=2,'seq'=4,'lab'=4] {'lab'}, dimensions={0}, use_global_device_ids=true | all-gather | bytes 491520 | tf_op jit(solution)/shard_map/all_gather | solution.py:80
  126.1 1.4 fusion.2
  127.6 4.2 %convolution_convert_fusion.1 = bf16[2304,256]{1,0:T(8,128)(2,1)} fusion(bf16[768,2304]{1,0:T(8,128)(2,1)} %copy-done.3, bf16[768,256]{1,0:T(8,128)(2,1)S(1)} %all_gather.6), kind=kOutput, calls=%fused_computation.5 | convolution fusion | flops 906559488 | bytes 5111808 | tf_op jit(solution)/shard_map/tc,te->ce/dot_general | solution.py:85
  131.9 4.3 %convolution_convert_fusion = bf16[2304,256]{1,0:T(8,128)(2,1)} fusion(bf16[768,2304]{1,0:T(8,128)(2,1)} %copy-done.2, bf16[768,256]{1,0:T(8,128)(2,1)S(1)} %all_gather.6), kind=kOutput, calls=%fused_computation.4 | convolution fusion | flops 906559488 | bytes 5111808 | tf_op jit(solution)/shard_map/tc,te->ce/dot_general | solution.py:86
  136.2 8.4 %psum.39 = f32[2]{0:T(128)S(1)} all-reduce(f32[2]{0:T(128)S(1)} %get-tuple-element.27), channel_id=1, replica_groups=mesh['grp'=2,'seq'=4,'lab'=4] {'lab'}, use_global_device_ids=true, to_apply=%region_9.11 | all-reduce | flops 2 | bytes 16 | tf_op jit(solution)/shard_map/psum | solution.py:55
  144.6 0.5 broadcast_multiply_fusion.1
  145.1 1.7 convolution_convert_fusion.2
  146.8 0.3 reduce-scatter.10.cloned.1.call-done
  147.1 1.7 copy.13
  148.8 27.2 %reduce-scatter.12.cloned.1.call-done = bf16[576,256]{1,0:T(8,128)(2,1)} async-done(((bf16[2304,256]{1,0:T(8,128)(2,1)}), bf16[576,256]{1,0:T(8,128)(2,1)}) %reduce-scatter.12.cloned.1.call-update) | async-done | bytes 294928 | tf_op jit(solution)/shard_map/reduce_scatter | solution.py:88
  176.0 28.7 %reduce-scatter.14.cloned.1.call-done = bf16[576,256]{1,0:T(8,128)(2,1)} async-done(((bf16[2304,256]{1,0:T(8,128)(2,1)}), bf16[576,256]{1,0:T(8,128)(2,1)}) %reduce-scatter.14.cloned.1.call-update) | async-done | bytes 294928 | tf_op jit(solution)/shard_map/reduce_scatter | solution.py:91
  (29 shorter events, 0.4 us)
Async XLA Ops:
  7.2 1.4 copy-start
  7.2 27.2 %reduce-scatter.6.cloned.1.call-start = ((), (), s32[]{:S(2)}) async-start(), calls=%async_computation.5 | async-start | bytes 491520 | tf_op jit(solution)/shard_map/reduce_scatter | solution.py:27
  11.0 99.4 %reduce-scatter.8.cloned.1.call-start = ((), (), s32[]{:S(2)}) async-start(), calls=%async_computation.6 | async-start | bytes 491520 | tf_op jit(solution)/shard_map/reduce_scatter | solution.py:70
  50.1 2.5 %copy-start.4 = (bf16[2304,256]{1,0:T(8,128)(2,1)S(1)}, bf16[2304,256]{1,0:T(8,128)(2,1)}, u32[]{:S(2)}) copy-start(bf16[2304,256]{1,0:T(8,128)(2,1)} %param.11) | copy-start | bytes 3538948
  52.6 5.0 %copy-start.1 = (f32[768,2304]{1,0:T(8,128)}, f32[768,2304]{1,0:T(8,128)S(1)}, u32[]{:S(2)}) copy-start(f32[768,2304]{1,0:T(8,128)S(1)} %fusion.17) | copy-start | bytes 21233668
  52.7 25.6 %copy-start.8 = (s32[2,2304]{1,0:T(2,128)S(1)}, s32[2,2304]{1,0:T(2,128)}, u32[]{:S(2)}) copy-start(s32[2,2304]{1,0:T(2,128)} %param.13) | copy-start | bytes 55300
  52.7 25.6 %copy-start.9 = (f32[2304]{0:T(1024)S(1)}, f32[2304]{0:T(1024)}, u32[]{:S(2)}) copy-start(f32[2304]{0:T(1024)} %param.12) | copy-start | bytes 27652
  79.4 7.9 %copy-start.5 = (bf16[2304,256]{1,0:T(8,128)(2,1)S(1)}, bf16[2304,256]{1,0:T(8,128)(2,1)}, u32[]{:S(2)}) copy-start(bf16[2304,256]{1,0:T(8,128)(2,1)} %param.10) | copy-start | bytes 3538948
  85.4 1.8 copy-start.3
  85.4 2.9 %copy-start.2 = (bf16[768,2304]{1,0:T(8,128)(2,1)}, bf16[768,2304]{1,0:T(8,128)(2,1)S(1)}, u32[]{:S(2)}) copy-start(bf16[768,2304]{1,0:T(8,128)(2,1)S(1)} %get-tuple-element.34) | copy-start | bytes 10616836
  88.3 22.1 %copy-start.7 = (bf16[192,256]{1,0:T(8,128)(2,1)S(1)}, bf16[192,256]{1,0:T(8,128)(2,1)}, u32[]{:S(2)}) copy-start(bf16[192,256]{1,0:T(8,128)(2,1)} %reduce-scatter.6.cloned.1.call-done) | copy-start | bytes 294916
  90.2 56.9 %reduce-scatter.10.cloned.1.call-start = ((), (), s32[]{:S(2)}) async-start(), calls=%async_computation.7 | async-start | bytes 655360 | tf_op jit(solution)/shard_map/reduce_scatter | solution.py:94
  127.6 48.4 %reduce-scatter.12.cloned.1.call-start = ((), (), s32[]{:S(2)}) async-start(), calls=%async_computation.8 | async-start | bytes 1474560 | tf_op jit(solution)/shard_map/reduce_scatter | solution.py:88
  131.8 13.3 %copy-start.6 = (bf16[1024,256]{1,0:T(8,128)(2,1)S(1)}, bf16[1024,256]{1,0:T(8,128)(2,1)}, u32[]{:S(2)}) copy-start(bf16[1024,256]{1,0:T(8,128)(2,1)} %param.9) | copy-start | bytes 1572868
  131.8 72.9 %reduce-scatter.14.cloned.1.call-start = ((), (), s32[]{:S(2)}) async-start(), calls=%async_computation.9 | async-start | bytes 1474560 | tf_op jit(solution)/shard_map/reduce_scatter | solution.py:91
Sparse Core Ops, SparseCore 0:
  11.1 23.2 reduce-scatter.5
  90.3 20.0 reduce-scatter.7
  127.7 19.3 reduce-scatter.9
  150.3 25.6 reduce-scatter.11
  179.0 25.7 reduce-scatter.13
where the time goes:
time: 212 us; the launch traced here: 211 us
  waiting for transfers between devices  99.1 us (47%)
  blocking collectives  57.2 us (27%)
  matrix products  24.2 us (11%)
  between operations  14.6 us (7%)
  other arithmetic  10.9 us (5%)
  local copies, waits for them, and re-layouts  5.01 us (2%)
    reduce_scatter x1, waiting for transfers between devices, per_device(): lax.psum_scatter(rounded(weight_part).astype(jnp.bfloat16), 'seq', scatte...  28.7 us
    reduce_scatter x1, waiting for transfers between devices, per_device(): lax.psum_scatter(rounded(query_part).astype(jnp.bfloat16), 'seq', scatter...  27.2 us
    reduce_scatter x1, waiting for transfers between devices, per_device(): lax.psum_scatter(jnp.dot(hidden, proj_weight, preferred_element_type=jnp....  22.6 us
    reduce_scatter x1, waiting for transfers between devices, per_device(): lax.psum_scatter((first + jnp.dot(value_grad, code_weight, preferred_elem...  20.2 us
    psum x2, blocking collectives, per_device(): lax.psum((jnp.sum(class_weight), jnp.sum(focal_value * class_weight[None,...  17.3 us
    all_gather x1, blocking collectives, per_device(): latent = lax.all_gather(latent_share, 'lab', axis=0, tiled=True)  14.8 us
    all_gather x1, blocking collectives, per_device(): pre_grad = lax.all_gather(pre_share_grad, 'lab', axis=0, tiled=True)  14.8 us
    psum x1, blocking collectives, per_device(): lax.psum(counts_local.astype(jnp.bfloat16), 'seq').astype(jnp.float32)  10.3 us
  transfers between devices with their start and end apart: 5, of which 5 were waited for; matrix products, arithmetic and copies ran while one was open for 6% of the time, Pallas kernels for 0%

commit v1 on v0

--- a/solution.py
+++ b/solution.py
@@ -43,7 +43,9 @@
     denominator, numerator, counted = (
         lax.psum((note_pick * den_local).astype(jnp.bfloat16), "seq").astype(jnp.float32),
         lax.psum((note_pick * num_local).astype(jnp.bfloat16), "seq").astype(jnp.float32),
-        lax.psum(counts_local.astype(jnp.bfloat16), "seq").astype(jnp.float32),
+        jnp.sum(lax.all_gather(counts_local.astype(jnp.bfloat16), "seq"), axis=0).astype(
+            jnp.float32
+        ),
     )
     mean_value = numerator / denominator
     logits = mean_value + code_bias[None, :]

time: 212 us -> 201 us (0.948)
  waiting for transfers between devices: 99.1 us -> 78 us
  blocking collectives: 57.2 us -> 67.3 us
    reduce_scatter x1, waiting for transfers between devices: 22.6 us -> 2.18 us  [per_device(): lax.psum_scatter(jnp.dot(hidden, proj_weight, preferred_element_type=jnp....]
    all_gather x0 -> x1, blocking collectives: none -> 6.16 us  [per_device(): lax.all_gather(counts_local.astype(jnp.bfloat16), 'seq')]
    psum x2, blocking collectives: 17.3 us -> 21.6 us  [per_device(): lax.psum((jnp.sum(class_weight), jnp.sum(focal_value * class_weight[None,...]
  transfers between devices with their start and end apart: 5 -> 5, of which waited for: 5 -> 5; matrix products, arithmetic and copies ran while one was open for 6% -> 7% of each run, Pallas kernels for 0% -> 0%
where the time goes in v1:
time: 201 us; the launch traced here: 200 us
  waiting for transfers between devices  78 us (39%)
  blocking collectives  67.3 us (33%)
  matrix products  24.2 us (12%)
  between operations  14.6 us (7%)
  other arithmetic  11 us (5%)
  local copies, waits for them, and re-layouts  5.01 us (2%)
    reduce_scatter x1, waiting for transfers between devices, per_device(): lax.psum_scatter(rounded(weight_part).astype(jnp.bfloat16), 'seq', scatte...  28.7 us
    reduce_scatter x1, waiting for transfers between devices, per_device(): lax.psum_scatter(rounded(query_part).astype(jnp.bfloat16), 'seq', scatter...  27.2 us
    psum x2, blocking collectives, per_device(): lax.psum((jnp.sum(class_weight), jnp.sum(focal_value * class_weight[None,...  21.6 us
    reduce_scatter x1, waiting for transfers between devices, per_device(): lax.psum_scatter((first + jnp.dot(value_grad, code_weight, preferred_elem...  19.1 us
    all_gather x1, blocking collectives, per_device(): pre_grad = lax.all_gather(pre_share_grad, 'lab', axis=0, tiled=True)  14.7 us
    all_gather x1, blocking collectives, per_device(): latent = lax.all_gather(latent_share, 'lab', axis=0, tiled=True)  14.6 us
    psum x1, blocking collectives, per_device(): lax.psum((note_pick * den_local).astype(jnp.bfloat16), 'seq')  10.3 us
    all_gather x1, blocking collectives, per_device(): lax.all_gather(counts_local.astype(jnp.bfloat16), 'seq')  6.16 us
  transfers between devices with their start and end apart: 5, of which 5 were waited for; matrix products, arithmetic and copies ran while one was open for 7% of the time, Pallas kernels for 0%

profile of v1, /device:TPU:0, one launch (start us, length us, event | category | flops | bytes accessed | tf_op | source)
XLA Modules:
  0.0 200.3 jit_solution(7117929174515972611)
XLA Ops:
  7.2 1.4 copy-done
  8.6 2.4 %convolution_convert_fusion.4 = bf16[768,256]{1,0:T(8,128)(2,1)} fusion(bf16[768,1024]{1,0:T(8,128)(2,1)S(1)} %copy-done, bf16[1024,256]{1,0:T(8,128)(2,1)} %param.9), kind=kOutput, calls=%fused_computation.11 | convolution fusion | flops 402849792 | bytes 2490368 | tf_op jit(solution)/shard_map/dot_general | solution.py:28
  11.0 0.7 convert_bitcast_fusion
  11.7 6.2 %all-gather = bf16[4,1,2304]{2,1,0:T(2,128)(2,1)S(1)} all-gather(bf16[1,1,2304]{2,1,0:T(2,128)(2,1)S(1)} %convert_bitcast_fusion), channel_id=1, replica_groups=mesh['grp'=2,'seq'=4,'lab'=4] {'seq'}, dimensions={0}, use_global_device_ids=true | all-gather | bytes 23040 | tf_op jit(solution)/shard_map/all_gather | solution.py:46
  18.0 0.6 negate_divide_fusion
  18.6 13.0 %psum.28 = f32[]{:T(128)} all-reduce(f32[]{:T(128)} %get-tuple-element.42), channel_id=1, replica_groups=mesh['grp'=2,'seq'=4,'lab'=4] {'lab'}, use_global_device_ids=true, to_apply=%region_2.3 | all-reduce | flops 1 | bytes 8 | tf_op jit(solution)/shard_map/psum | solution.py:57
  32.4 2.2 %reduce-scatter.6.cloned.1.call-done = bf16[192,256]{1,0:T(8,128)(2,1)} async-done(((bf16[768,256]{1,0:T(8,128)(2,1)}), bf16[192,256]{1,0:T(8,128)(2,1)}) %reduce-scatter.6.cloned.1.call-update) | async-done | bytes 98320 | tf_op jit(solution)/shard_map/reduce_scatter | solution.py:27
  34.5 0.9 tanh_convert_fusion
  35.5 14.6 %all_gather.11 = bf16[768,256]{1,0:T(8,128)(2,1)S(1)} all-gather(bf16[192,256]{1,0:T(8,128)(2,1)S(1)} %tanh_convert_fusion), channel_id=1, replica_groups=mesh['grp'=2,'seq'=4,'lab'=4] {'lab'}, dimensions={0}, use_global_device_ids=true | all-gather | bytes 491520 | tf_op jit(solution)/shard_map/all_gather | solution.py:34
  50.1 2.5 %fusion.17 = f32[768,2304]{1,0:T(8,128)S(1)} fusion(bf16[768,256]{1,0:T(8,128)(2,1)S(1)} %all_gather.11, bf16[2304,256]{1,0:T(8,128)(2,1)} %param.10), kind=kOutput, calls=%fused_computation.52 | convolution fusion | flops 905969664 | bytes 8650752 | tf_op jit(solution)/shard_map/te,ce->tc/dot_general | solution.py:35
  52.6 4.8 %multiply_reduce_fusion = (f32[2304]{0:T(1024)S(1)}, f32[2304]{0:T(1024)S(1)}, f32[768,2304]{1,0:T(8,128)}) fusion(f32[768,2304]{1,0:T(8,128)S(1)} %fusion.17, bf16[768,256]{1,0:T(8,128)(2,1)S(1)} %all_gather.11, bf16[2304,256]{1,0:T(8,128)(2,1)S(1)} %copy-done.4), kind=kOutput, calls=%fused_computation.2 | convolution fusion | flops 911273472 | bytes 15747072 | tf_op jit(solution)/shard_map/te,ce->tc/dot_general | solution.py:36
  57.4 0.2 copy-done.1
  57.6 10.3 %all-reduce = (bf16[2,2304]{1,0:T(2,128)(2,1)S(1)}, bf16[2,2304]{1,0:T(2,128)(2,1)S(1)}) all-reduce(bf16[2,2304]{1,0:T(2,128)(2,1)S(1)} %get-tuple-element.44, bf16[2,2304]{1,0:T(2,128)(2,1)S(1)} %get-tuple-element.43), channel_id=1, replica_groups=mesh['grp'=2,'seq'=4,'lab'=4] {'seq'}, use_global_device_ids=true, to_apply=%region_7.8 | all-reduce | flops 9216 | bytes 36864 | tf_op jit(solution)/shard_map/psum | solution.py:44
  67.9 0.2 fusion.14
  68.1 0.8 fusion.16
  68.9 6.0 %fusion = (bf16[768,2304]{1,0:T(8,128)(2,1)S(1)}, bf16[768,2304]{1,0:T(8,128)(2,1)S(1)}) fusion(f32[2304]{0:T(1024)S(1)} %get-tuple-element.29, f32[2304]{0:T(1024)S(1)} %get-tuple-element.32, f32[768,2304]{1,0:T(8,128)} %copy-done.1, f32[768,2304]{1,0:T(8,128)} %get-tuple-element.45, f32[2304]{0:T(1024)S(1)} %get-tuple-element.34), kind=kLoop, calls=%fused_computation.6 | loop fusion | flops 10616832 | bytes 21261312 | tf_op jit(solution)/shard_map/convert_element_type | solution.py:69
  75.0 1.8 copy-done.3
  76.8 1.1 fusion.18
  77.9 1.8 fusion.1
  79.8 19.1 %reduce-scatter.8.cloned.1.call-done = bf16[192,256]{1,0:T(8,128)(2,1)} async-done(((bf16[768,256]{1,0:T(8,128)(2,1)}), bf16[192,256]{1,0:T(8,128)(2,1)}) %reduce-scatter.8.cloned.1.call-update) | async-done | bytes 98320 | tf_op jit(solution)/shard_map/reduce_scatter | solution.py:72
  99.0 0.9 multiply_convert_fusion.1
  99.9 14.7 %all_gather.12 = bf16[768,256]{1,0:T(8,128)(2,1)S(1)} all-gather(bf16[192,256]{1,0:T(8,128)(2,1)S(1)} %multiply_convert_fusion.1), channel_id=1, replica_groups=mesh['grp'=2,'seq'=4,'lab'=4] {'lab'}, dimensions={0}, use_global_device_ids=true | all-gather | bytes 491520 | tf_op jit(solution)/shard_map/all_gather | solution.py:82
  114.6 1.4 fusion.2
  116.2 4.2 %convolution_convert_fusion.1 = bf16[2304,256]{1,0:T(8,128)(2,1)} fusion(bf16[768,2304]{1,0:T(8,128)(2,1)} %copy-done.3, bf16[768,256]{1,0:T(8,128)(2,1)S(1)} %all_gather.11), kind=kOutput, calls=%fused_computation.5 | convolution fusion | flops 906559488 | bytes 5111808 | tf_op jit(solution)/shard_map/tc,te->ce/dot_general | solution.py:87
  120.4 4.3 %convolution_convert_fusion = bf16[2304,256]{1,0:T(8,128)(2,1)} fusion(bf16[768,2304]{1,0:T(8,128)(2,1)} %copy-done.2, bf16[768,256]{1,0:T(8,128)(2,1)S(1)} %all_gather.11), kind=kOutput, calls=%fused_computation.4 | convolution fusion | flops 906559488 | bytes 5111808 | tf_op jit(solution)/shard_map/tc,te->ce/dot_general | solution.py:88
  124.7 8.5 %psum.31 = f32[2]{0:T(128)S(1)} all-reduce(f32[2]{0:T(128)S(1)} %get-tuple-element.33), channel_id=1, replica_groups=mesh['grp'=2,'seq'=4,'lab'=4] {'lab'}, use_global_device_ids=true, to_apply=%region_9.11 | all-reduce | flops 2 | bytes 16 | tf_op jit(solution)/shard_map/psum | solution.py:57
  133.3 0.5 broadcast_multiply_fusion.1
  133.8 1.8 convolution_convert_fusion.2
  135.5 0.6 reduce-scatter.10.cloned.1.call-done
  136.1 1.7 copy.14
  137.8 27.2 %reduce-scatter.12.cloned.1.call-done = bf16[576,256]{1,0:T(8,128)(2,1)} async-done(((bf16[2304,256]{1,0:T(8,128)(2,1)}), bf16[576,256]{1,0:T(8,128)(2,1)}) %reduce-scatter.12.cloned.1.call-update) | async-done | bytes 294928 | tf_op jit(solution)/shard_map/reduce_scatter | solution.py:90
  165.0 28.7 %reduce-scatter.14.cloned.1.call-done = bf16[576,256]{1,0:T(8,128)(2,1)} async-done(((bf16[2304,256]{1,0:T(8,128)(2,1)}), bf16[576,256]{1,0:T(8,128)(2,1)}) %reduce-scatter.14.cloned.1.call-update) | async-done | bytes 294928 | tf_op jit(solution)/shard_map/reduce_scatter | solution.py:93
  (31 shorter events, 0.5 us)
Async XLA Ops:
  7.2 1.4 copy-start
  7.2 27.4 %reduce-scatter.6.cloned.1.call-start = ((), (), s32[]{:S(2)}) async-start(), calls=%async_computation.5 | async-start | bytes 491520 | tf_op jit(solution)/shard_map/reduce_scatter | solution.py:27
  11.0 88.0 %reduce-scatter.8.cloned.1.call-start = ((), (), s32[]{:S(2)}) async-start(), calls=%async_computation.6 | async-start | bytes 491520 | tf_op jit(solution)/shard_map/reduce_scatter | solution.py:72
  50.1 2.5 %copy-start.4 = (bf16[2304,256]{1,0:T(8,128)(2,1)S(1)}, bf16[2304,256]{1,0:T(8,128)(2,1)}, u32[]{:S(2)}) copy-start(bf16[2304,256]{1,0:T(8,128)(2,1)} %param.11) | copy-start | bytes 3538948
  52.5 5.0 %copy-start.1 = (f32[768,2304]{1,0:T(8,128)}, f32[768,2304]{1,0:T(8,128)S(1)}, u32[]{:S(2)}) copy-start(f32[768,2304]{1,0:T(8,128)S(1)} %fusion.17) | copy-start | bytes 21233668
  52.6 15.3 %copy-start.8 = (s32[2,2304]{1,0:T(2,128)S(1)}, s32[2,2304]{1,0:T(2,128)}, u32[]{:S(2)}) copy-start(s32[2,2304]{1,0:T(2,128)} %param.13) | copy-start | bytes 55300
  52.6 15.3 %copy-start.9 = (f32[2304]{0:T(1024)S(1)}, f32[2304]{0:T(1024)}, u32[]{:S(2)}) copy-start(f32[2304]{0:T(1024)} %param.12) | copy-start | bytes 27652
  68.9 7.9 %copy-start.5 = (bf16[2304,256]{1,0:T(8,128)(2,1)S(1)}, bf16[2304,256]{1,0:T(8,128)(2,1)}, u32[]{:S(2)}) copy-start(bf16[2304,256]{1,0:T(8,128)(2,1)} %param.10) | copy-start | bytes 3538948
  75.0 1.8 copy-start.3
  75.0 2.9 %copy-start.2 = (bf16[768,2304]{1,0:T(8,128)(2,1)}, bf16[768,2304]{1,0:T(8,128)(2,1)S(1)}, u32[]{:S(2)}) copy-start(bf16[768,2304]{1,0:T(8,128)(2,1)S(1)} %get-tuple-element.39) | copy-start | bytes 10616836
  77.9 21.1 %copy-start.7 = (bf16[192,256]{1,0:T(8,128)(2,1)S(1)}, bf16[192,256]{1,0:T(8,128)(2,1)}, u32[]{:S(2)}) copy-start(bf16[192,256]{1,0:T(8,128)(2,1)} %reduce-scatter.6.cloned.1.call-done) | copy-start | bytes 294916
  79.8 56.3 %reduce-scatter.10.cloned.1.call-start = ((), (), s32[]{:S(2)}) async-start(), calls=%async_computation.7 | async-start | bytes 655360 | tf_op jit(solution)/shard_map/reduce_scatter | solution.py:96
  116.1 48.9 %reduce-scatter.12.cloned.1.call-start = ((), (), s32[]{:S(2)}) async-start(), calls=%async_computation.8 | async-start | bytes 1474560 | tf_op jit(solution)/shard_map/reduce_scatter | solution.py:90
  120.3 13.4 %copy-start.6 = (bf16[1024,256]{1,0:T(8,128)(2,1)S(1)}, bf16[1024,256]{1,0:T(8,128)(2,1)}, u32[]{:S(2)}) copy-start(bf16[1024,256]{1,0:T(8,128)(2,1)} %param.9) | copy-start | bytes 1572868
  120.3 73.4 %reduce-scatter.14.cloned.1.call-start = ((), (), s32[]{:S(2)}) async-start(), calls=%async_computation.9 | async-start | bytes 1474560 | tf_op jit(solution)/shard_map/reduce_scatter | solution.py:93
Sparse Core Ops, SparseCore 0:
  11.1 23.4 reduce-scatter.5
  79.9 19.0 reduce-scatter.7
  116.2 19.8 reduce-scatter.9
  139.3 25.6 reduce-scatter.11
  168.0 25.7 reduce-scatter.13
